TPU v7x, 32 devices: a whole 2x2x4 slice. The times are simulated.
32 devices in a mesh: tenant: 8 (over z, core), row: 4 (over y, x).
Axes of the slice: x: 2, y: 2, z: 4, core: 2. Of those that a mesh axis runs over, the one named last changes fastest.
Arguments:
- b_factors: float32 [64, 16, 8192], P('tenant', None, 'row'), may hold values from -6 to 6
- a_factors: float32 [64, 16, 8192], P('tenant', None, 'row'), may hold values from -6 to 6
- u_start: float32 [8192, 256], P('row'), may hold values from -0.0625 to 0.0625
- v_start: float32 [8192, 256], P('row'), may hold values from -0.0625 to 0.0625
Outputs:
- u_scaled: float32 [8192, 256], P('row')
- v_scaled: float32 [8192, 256], P('row')
- core_left: float32 [64, 16, 256], P('tenant')
- core_right: float32 [64, 16, 256], P('tenant')
All inputs are finite; a program needn't handle non-finite values.
Results may differ from a plain program's by a relative error of at most 0.0003.
Values sent between devices are 32-bit elements; how exact they have to be, the bound alone decides.
A program may use at most 64 MiB of HBM per device.

v0:
```python
import functools
import math

import jax
import jax.numpy as jnp
from jax import lax
from jax.experimental import pallas as pl
from jax.experimental.pallas import tpu as pltpu
from jax.sharding import PartitionSpec as P

HIGH = lax.Precision.HIGHEST
MESH = pl.DeviceIdType.MESH
VMEM = pl.BlockSpec(memory_space=pltpu.VMEM)
ANY = pl.BlockSpec(memory_space=pl.ANY)
HBM = pl.BlockSpec(memory_space=pltpu.HBM)
BLK = 64
OUT = 4
WIDE = 128
ROOM = 44 << 20
SMALL = 2 << 20
GROUP = 4


def mm(x, y, cx, cy):
    return lax.dot_general(x, y, (((cx,), (cy,)), ((), ())), precision=HIGH, preferred_element_type=jnp.float32)


def split(x):
    top = x.astype(jnp.bfloat16)
    return top, (x - top.astype(jnp.float32)).astype(jnp.bfloat16)


def dot3(x, y, cx, cy):
    (xt, xl), (yt, yl) = x, y
    dot = functools.partial(lax.dot_general, dimension_numbers=(((cx,), (cy,)), ((), ())),
                            preferred_element_type=jnp.float32)
    return dot(xt, yt) + (dot(xt, yl) + dot(xl, yt))


def mm3(x, y, cx, cy):
    return dot3(split(x), split(y), cx, cy)


def remote(src, dst, send, recv, device):
    return pltpu.make_async_remote_copy(
        src_ref=src, dst_ref=dst, send_sem=send, recv_sem=recv, device_id=device, device_id_type=MESH)


def signal(device):
    pl.semaphore_signal(pltpu.get_barrier_semaphore(), inc=1, device_id=device, device_id_type=MESH)


def bits_of(n_row):
    bits = n_row.bit_length() - 1
    assert 1 << bits == n_row
    return bits


def row_partner(bit):
    row = lax.axis_index("row")
    return row + (1 << bit) - 2 * (1 << bit) * (lax.rem(row // (1 << bit), 2))


def row_parts(bits, acc, got, send, recv, base, size):
    half = size // 2

    def copy(step, part):
        bit = (step + part) % bits
        rows = pl.ds(base + part * half, half)
        at = base // size
        return remote(acc.at[step, rows], got.at[step, rows], send.at[at, step, part], recv.at[at, step, part],
                      {"row": row_partner(bit)})

    def begin():
        for part in range(2):
            copy(0, part).start()

    def meet(step):
        for part in range(2):
            rows = pl.ds(base + part * half, half)
            copy(step, part).wait_recv()
            acc[step + 1, rows, :] = acc[step, rows, :] + got[step, rows, :]
            if step + 1 < bits:
                copy(step + 1, part).start()

    def end():
        for step in range(bits):
            for part in range(2):
                copy(step, part).wait_send()

    return begin, meet, end


def factor_block(block):
    n = block.shape[0]
    eye = (lax.broadcasted_iota(jnp.int32, (n, n), 0) == lax.broadcasted_iota(jnp.int32, (n, n), 1)).astype(block.dtype)
    full = jnp.concatenate([block, eye], axis=1)
    groups = [full[8 * g:8 * g + 8, :] for g in range(n // 8)]
    sub = lax.broadcasted_iota(jnp.int32, (8, 2 * n), 0)
    for g in range(n // 8):
        cols = [[jnp.broadcast_to(groups[h][:, 8 * g + c:8 * g + c + 1], (8, 2 * n)) for c in range(8)]
                for h in range(g, n // 8)]
        heads = [[cols[0][c][r:r + 1, :] for c in range(8)] for r in range(8)]
        lines = [groups[g][r:r + 1, :] for r in range(8)]
        invs = []
        for p in range(8):
            inv = 1.0 / heads[p][p]
            invs.append(inv)
            for r in range(p + 1, 8):
                factor = heads[r][p] * inv
                lines[r] = lines[r] - factor * lines[p]
                for c in range(p + 1, 8):
                    heads[r][c] = heads[r][c] - factor * heads[p][c]
        for h in range(g + 1, n // 8):
            col = cols[h - g]
            total = groups[h]
            for p in range(8):
                factor = col[p] * invs[p]
                total = total - factor * lines[p]
                for c in range(p + 1, 8):
                    col[c] = col[c] - factor * heads[p][c]
            groups[h] = total
        group = jnp.broadcast_to(lines[0], (8, 2 * n))
        for r in range(1, 8):
            group = jnp.where(sub == r, lines[r], group)
        groups[g] = group
    full = jnp.concatenate(groups, axis=0)
    diag = jnp.sum(full[:, :n] * eye, axis=1, keepdims=True)
    return full[:, n:] * lax.rsqrt(diag)


def sweep_kernel(bits, chain, rank, scale, b_hbm, a_hbm, u_hbm, v_hbm, fu_hbm, fv_hbm, fleft_ref, fright_ref,
                 f, x, acc, got, own, cs, rs, ctop, clow, mtop, mlow, m, gpart, gmate, gacc, ggot, gfin, lp, lmate, lgot, lcross, lfull, lout,
                 tab, linv_ref, lout_ref, load, row_send, row_recv, own_send, own_recv, own_here, *more):
    c_sems, r_sems = more[:6], more[6:12]
    (gm_send, gm_recv, g_send, g_recv, gf_send, gf_recv, go_send, lm_send, lm_recv, lc_send, lc_recv, rs_send, rs_recv,
     ag_send, ag_recv, lh_send, lh_recv, lo_send, lo_recv, mo_send, m_recv, mp_send, mr_send, mf_send, store) = more[12:]
    tenant, row = lax.axis_index("tenant"), lax.axis_index("row")
    core, place = lax.rem(tenant, 2), tenant // 2
    nt, n_row = 2 * chain, 1 << bits
    low = chain // 2 - 1
    outs = chain // 2 - 1
    side = place // (chain // 2)
    is_mid = jnp.logical_or(place == low, place == low + 1)
    is_out = jnp.logical_not(is_mid)
    is_hub = jnp.logical_and(is_mid, core == 1)
    is_sub = jnp.logical_and(is_mid, core == 0)
    mate = {"tenant": tenant + 1 - 2 * core}
    across = {"tenant": 2 * (2 * low + 1 - place) + core}
    nb = bits + 1
    rows, width = f.shape[1:]
    k = x.shape[2]
    kh = k // 2
    wq = width // 4
    half = nt * rows // 2
    piece = half // n_row
    mine = 2 * side + core

    def outer(j):
        return (1 - side) * (low - 1 - j) + side * (low + 2 + j)

    def out_device(j):
        return {"tenant": 2 * outer(j) + core}

    def neighbour(d):
        to = row
        for bit in range(bits):
            if d >> bit & 1:
                to = to + (1 << bit) - 2 * (1 << bit) * lax.rem(to // (1 << bit), 2)
        return to

    pairs = ((b_hbm, f.at[0]), (u_hbm, x.at[0]), (a_hbm, f.at[1]), (v_hbm, x.at[1]))
    loads = [pltpu.make_async_copy(src, dst, load.at[i]) for i, (src, dst) in enumerate(pairs)]
    for copy in loads:
        copy.start()
    for d in range(1, nt):
        signal({"tenant": lax.rem(tenant + d, nt)})
    for d in range(1, n_row):
        signal({"row": lax.rem(row + d, n_row)})

    @pl.when(is_mid)
    def _():
        for d in range(1, n_row):
            signal({"tenant": 2 * (2 * low + 1 - place) + core, "row": lax.rem(row + d, n_row)})

    def ship(fac, q, lines=None):
        cols = pl.ds(q * wq, wq)
        target = 2 * (low + q // 2) + q % 2
        lines = lines or pl.ds(0, rows)
        sent = remote(f.at[fac, lines, cols], own.at[fac, tenant, lines], own_send.at[fac, q], own_recv.at[fac, tenant],
                      {"tenant": target})
        kept = pltpu.make_async_copy(f.at[fac, :, cols], own.at[fac, tenant], own_here.at[fac])
        return target, sent, kept

    def near(target):
        return target // 2 // (chain // 2) == side

    def far(target):
        return target // 2 // (chain // 2) != side

    def ship_all(fac, some, cores=(0, 1), lines=None):
        for q in [2 * h + c for h in range(2) for c in cores]:
            target, sent, kept = ship(fac, q, lines)

            @pl.when(jnp.logical_and(tenant != target, some(target)))
            def _(sent=sent):
                sent.start()

            if some is not far:
                @pl.when(tenant == target)
                def _(kept=kept):
                    kept.start()

    def ship_end(fac):
        for q in range(4):
            target, sent, kept = ship(fac, q)

            @pl.when(tenant != target)
            def _(sent=sent):
                sent.wait_send()

    def own_wait(fac):
        cols = pl.ds(pl.multiple_of(mine * wq, wq), wq)
        pltpu.make_async_copy(f.at[fac, :, cols], own.at[fac, tenant], own_here.at[fac]).wait()

        def one(i, _):
            @pl.when(i != tenant)
            def _():
                remote(own.at[fac, i], own.at[fac, i], own_send.at[fac, 0], own_recv.at[fac, i], mate).wait_recv()

            return 0

        lax.fori_loop(0, nt, one, 0)

    top, bottom = pl.ds(0, rows // 2), pl.ds(rows // 2, rows - rows // 2)
    tile = 512 if width % 512 == 0 else width
    acc[0] = jnp.zeros_like(acc[0])
    parts = [row_parts(bits, acc, got, row_send, row_recv, fac * rows, rows) for fac in range(2)]
    for fac in range(2):
        loads[2 * fac].wait()
        if fac == 0:
            pl.semaphore_wait(pltpu.get_barrier_semaphore(), nt - 1 + (n_row - 1) * (1 + is_mid.astype(jnp.int32)))

            ship_all(0, near)

            @pl.when(is_mid)
            def _():
                ship_all(0, far)

            @pl.when(is_out)
            def _():
                ship_all(0, far, (1,), top)

        loads[2 * fac + 1].wait()

        def step(i, _, fac=fac):
            cols = pl.ds(pl.multiple_of(i * tile, tile), tile)
            acc[0, pl.ds(fac * rows, rows), :] += mm3(f[fac, :, cols], x[fac, cols, :], 1, 0)
            return 0

        lax.fori_loop(0, width // tile, step, 0)
        parts[fac][0]()
    for at in range(bits):
        for fac in range(2):
            parts[fac][1](at)

    same = lax.broadcasted_iota(jnp.int32, (rows, rows), 0) // rank == lax.broadcasted_iota(
        jnp.int32, (rows, rows), 1) // rank
    rq = rows // n_row
    strip = pl.ds(pl.multiple_of(row * rq, 8), rq)
    below = acc[bits, pl.ds(pl.multiple_of(rows + row * rq, 8), rq), :]
    own_rank = (row * rq + lax.broadcasted_iota(jnp.int32, (rq, rows), 0)) // rank == lax.broadcasted_iota(
        jnp.int32, (rq, rows), 1) // rank
    weight = jnp.where(own_rank, mm(below, acc[bits, rows:, :], 1, 1), 0.0)
    cs[0, place, core, strip, :] = mm(weight, acc[bits, :rows, :], 1, 0)
    rs[place, core, strip, :] = below

    def hand(buf, sems, hop):
        to = low + hop
        part = buf.at[place, core, strip]
        return to, remote(part, part, sems[0].at[hop], sems[1].at[place], {"tenant": 2 * to + core})

    def hand_all(buf, sems):
        for hop in range(2):
            to, sent = hand(buf, sems, hop)

            @pl.when(place != to)
            def _(sent=sent):
                sent.start()

    def spread_copy(buf, sems, d):
        to = neighbour(d)
        part = buf.at[:, core, strip]
        return to, remote(part, part, sems[2].at[d - 1], sems[3].at[row], {"row": to})

    def spread_mate(buf, sems):
        part = buf.at[:, core]
        return remote(part, part, sems[4].at[0], sems[5].at[0], mate)

    def spread_begin(buf, sems):
        def take(i, _):
            @pl.when(i != place)
            def _():
                part = buf.at[i, core, strip]
                remote(part, part, sems[0].at[0], sems[1].at[i], mate).wait_recv()

            return 0

        lax.fori_loop(0, chain, take, 0)
        for d in range(1, n_row):
            spread_copy(buf, sems, d)[1].start()

    def spread_meet(buf, sems):
        for d in range(1, n_row):
            to = spread_copy(buf, sems, d)[0]
            part = buf.at[:, core, pl.ds(pl.multiple_of(to * rq, 8), rq)]
            remote(part, part, sems[2].at[0], sems[3].at[to], mate).wait_recv()
        spread_mate(buf, sems).start()

    def spread_rest(buf, sems):
        part = buf.at[:, 1 - core]
        remote(part, part, sems[4].at[0], sems[5].at[0], mate).wait_recv()

    def spread_end(buf, sems):
        for hop in range(2):
            to, sent = hand(buf, sems, hop)

            @pl.when(place != to)
            def _(sent=sent):
                sent.wait_send()

        @pl.when(is_mid)
        def _():
            for d in range(1, n_row):
                spread_copy(buf, sems, d)[1].wait_send()
            spread_mate(buf, sems).wait_send()

    first = cs.at[0]
    hand_all(first, c_sems)

    hand_all(rs, r_sems)

    @pl.when(is_out)
    def _():
        ship_all(0, far, (1,), bottom)
        ship_all(0, far, (0,))
        ship_all(1, far)

    ship_all(1, near)

    for fac in range(2):
        parts[fac][2]()

    def quarter_out(ph, j):
        return remote(m.at[ph, mine], m.at[ph, mine], mo_send.at[ph, j], m_recv.at[ph, mine], out_device(j))

    def quarter_across(ph, c):
        part = m.at[ph, 2 * side + c]
        return remote(part, part, mp_send.at[ph, c], m_recv.at[ph, 2 * side + c], across)

    def quarter_relay(ph, c, j):
        at = 2 * (1 - side) + c
        return remote(m.at[ph, at], m.at[ph, at], mr_send.at[ph, c, j], m_recv.at[ph, at], out_device(j))

    def quarter_mate(ph, at):
        return remote(m.at[ph, at], m.at[ph, at], mf_send.at[ph, at], m_recv.at[ph, at], mate)

    def quarter_wait(ph, at):
        remote(m.at[ph, at], m.at[ph, at], mp_send.at[ph, 0], m_recv.at[ph, at], mate).wait_recv()

    def cross(ph):
        quarter_across(ph, 0).start()
        quarter_wait(ph, 2 * side + 1)
        quarter_across(ph, 1).start()

    distant = [2 * (1 - side) + c for c in range(2)]

    def relay(ph, c):
        quarter_wait(ph, distant[c])
        quarter_mate(ph, distant[c]).start()
        if c == 0:
            for j in range(outs):
                quarter_relay(ph, c, j).start()

    def relay_hub(ph):
        quarter_wait(ph, distant[1])
        for j in range(outs):
            quarter_relay(ph, 1, j).start()

    def gram_mate(ph):
        return remote(gpart.at[ph], gmate.at[ph], gm_send.at[ph], gm_recv.at[ph], mate)

    def gram_copy(ph, at, part):
        dim = (at + part) % nb
        device = across if dim == bits else {"row": row_partner(dim)}
        return remote(gacc.at[ph, at, part], ggot.at[ph, at, part], g_send.at[ph, at, part], g_recv.at[ph, at, part], device)

    def gram_down(ph):
        return remote(gfin.at[ph], gfin.at[ph], gf_send.at[ph], gf_recv.at[ph], mate)

    def gram_out(ph, j):
        return remote(gfin.at[ph], gfin.at[ph], go_send.at[ph, j], gf_recv.at[ph], out_device(j))

    def gram_meet(ph, at):
        for part in range(3):
            gram_copy(ph, at, part).wait_recv()
            total = gacc[ph, at, part] + ggot[ph, at, part]
            if at + 1 < nb:
                gacc[ph, at + 1, part] = total
                gram_copy(ph, at + 1, part).start()
            else:
                gfin[ph, part] = total

    def left_mate(ph):
        there = pl.ds(pl.multiple_of((1 - core) * half, half), half)
        return remote(lp.at[ph, there], lmate.at[ph], lm_send.at[ph], lm_recv.at[ph], mate)

    def piece_at(at):
        return pl.ds(pl.multiple_of(core * half + at * piece, 8), piece)

    def left_copy(ph, d):
        to = neighbour(d)
        return remote(lp.at[ph, piece_at(to)], lgot.at[ph, row], rs_send.at[ph, d - 1], rs_recv.at[ph, row], {"row": to})

    def left_cross(ph):
        return remote(lp.at[ph, piece_at(row)], lcross.at[ph], lc_send.at[ph], lc_recv.at[ph], across)

    def left_share(ph, d):
        part = lfull.at[ph, piece_at(row)]
        return remote(part, part, ag_send.at[ph, d - 1], ag_recv.at[ph, row], {"row": neighbour(d)})

    def left_half(ph):
        here = pl.ds(pl.multiple_of(core * half, half), half)
        return remote(lfull.at[ph, here], lfull.at[ph, here], lh_send.at[ph], lh_recv.at[ph], mate)

    def left_out(ph, j, c):
        to = 2 * outer(j) + c
        here = pl.ds(pl.multiple_of(to * rows, rows), rows)
        return remote(lfull.at[ph, here], lout.at[ph], lo_send.at[ph, j, c], lo_recv.at[ph], {"tenant": to})

    def left_sum(ph):
        for d in range(1, n_row):
            to = neighbour(d)
            remote(lgot.at[ph, to], lgot.at[ph, to], rs_send.at[ph, 0], rs_recv.at[ph, to], mate).wait_recv()
        total = lp[ph, piece_at(row), :]
        for at in range(n_row):
            total += lgot[ph, at]
        lp[ph, piece_at(row), :] = total
        left_cross(ph).start()

    def left_join(ph):
        left_cross(ph).wait_recv()
        lfull[ph, piece_at(row), :] = lp[ph, piece_at(row), :] + lcross[ph]
        for d in range(1, n_row):
            left_share(ph, d).start()

    lgot[0, row] = jnp.zeros_like(lgot[0, 0])
    lgot[1, row] = jnp.zeros_like(lgot[1, 0])

    def body(ph, _):
        @pl.when(is_mid)
        def _():
            @pl.when(ph == 0)
            def _():
                spread_begin(first, c_sems)
                spread_meet(first, c_sems)
                spread_rest(first, c_sems)

            @pl.when(jnp.logical_and(ph == 1, core == 0))
            def _():
                relay(0, 0)

            own_wait(ph)
            coeffs = cs[ph].reshape(nt * rows, k)
            ctop[...], clow[...] = split(coeffs)

            def columns(j, _):
                cols = pl.ds(pl.multiple_of(j * WIDE, WIDE), WIDE)
                here = pl.ds(pl.multiple_of(j * WIDE, WIDE), WIDE)
                block = own[ph, :, :, cols].reshape(nt * rows, WIDE)
                total = dot3(split(block), (ctop[...], clow[...]), 0, 0)
                m[ph, mine, here, :] = total
                mtop[here, :], mlow[here, :] = split(total)
                return 0

            lax.fori_loop(0, wq // WIDE, columns, 0)
            for j in range(outs):
                quarter_out(ph, j).start()
            quarter_mate(ph, mine).start()
            mq = m.at[ph, mine]
            upper = mm(mq[:, :kh], mq[...], 0, 0)
            grams = (upper[:, :kh], upper[:, kh:], mm(mq[:, kh:], mq[:, kh:], 0, 0))
            for part in range(3):
                gpart[ph, part] = grams[part]

            @pl.when(core == 0)
            def _():
                gram_mate(ph).start()

            @pl.when(core == 1)
            def _():
                gram_mate(ph).wait_recv()
                for part in range(3):
                    gacc[ph, 0, part] = gpart[ph, part] + gmate[ph, part]
                    gram_copy(ph, 0, part).start()

            def lefts(i, _):
                here = pl.ds(pl.multiple_of(i * rows, rows), rows)
                lp[ph, here, :] = dot3(split(own[ph, i]), (mtop[...], mlow[...]), 1, 0)
                return 0

            lax.fori_loop(0, nt, lefts, 0)
            left_mate(ph).start()

            order = sorted(range(1, n_row), key=lambda d: (bin(d).count("1"), d))
            share = -(-len(order) // nb)

            def lefts_ready():
                left_mate(ph).wait_recv()
                here = pl.ds(pl.multiple_of(core * half, half), half)
                lp[ph, here, :] += lmate[ph]

            @pl.when(core == 1)
            def _():
                gram_meet(ph, 0)
                lefts_ready()

                for at in range(nb):
                    if at:
                        gram_meet(ph, at)
                    if at == nb - 1:
                        gram_down(ph).start()
                        for j in range(outs):
                            gram_out(ph, j).start()
                    for d in order[at * share:(at + 1) * share]:
                        left_copy(ph, d).start()

                @pl.when(ph == 1)
                def _():
                    relay_hub(0)

            @pl.when(core == 0)
            def _():
                @pl.when(ph == 1)
                def _():
                    cross(1)

                lefts_ready()

                for d in order:
                    left_copy(ph, d).start()

                @pl.when(ph == 1)
                def _():
                    relay(0, 1)
                    relay(1, 0)

                @pl.when(ph == 0)
                def _():
                    spread_begin(rs, r_sems)
                    ship_all(1, far)

                gram_down(ph).wait_recv()

            @pl.when(jnp.logical_and(ph == 0, core == 1))
            def _():
                spread_begin(rs, r_sems)

            left_sum(ph)

            @pl.when(jnp.logical_and(ph == 0, core == 1))
            def _():
                ship_all(1, far)

        @pl.when(is_out)
        def _():
            gram_down(ph).wait_recv()

            @pl.when(core == 1)
            def _():
                gram_down(ph).start()

        tab[:kh, :kh] = gfin[ph, 0]
        tab[:kh, kh:k] = gfin[ph, 1]
        tab[kh:, kh:k] = gfin[ph, 2]
        tab[:, k:] = (lax.broadcasted_iota(jnp.int32, (k, k), 0) == lax.broadcasted_iota(
            jnp.int32, (k, k), 1)).astype(jnp.float32)
        for at in range(0, k, BLK):
            end = at + BLK
            small = factor_block(tab[at:end, at:end])
            done = mm(small, tab[at:end, at:], 1, 0)
            tab[at:end, at:] = done
            if end < k:
                tab[end:, end:] -= mm(done[:, end - at:k - at], done[:, end - at:], 0, 0)
            if at == BLK:
                @pl.when(jnp.logical_and(is_mid, ph == 0))
                def _():
                    left_join(0)

                @pl.when(jnp.logical_and(is_hub, ph == 1))
                def _():
                    relay_hub(1)
            if at == 0:
                @pl.when(jnp.logical_and(is_mid, ph == 1))
                def _():
                    @pl.when(core == 0)
                    def _():
                        relay(1, 1)

                    left_join(1)
            if at == 2 * BLK:
                @pl.when(is_mid)
                def _():
                    @pl.when(ph == 0)
                    def _():
                        spread_meet(rs, r_sems)

                        @pl.when(core == 0)
                        def _():
                            cross(0)
        linv_ref[ph] = tab[:, k:]

        @pl.when(is_mid)
        def _():
            for d in range(1, n_row):
                part = lfull.at[ph, piece_at(neighbour(d))]
                remote(part, part, ag_send.at[ph, 0], ag_recv.at[ph, neighbour(d)], mate).wait_recv()
            left_half(ph).start()
            left_half(ph).wait_recv()

            @pl.when(ph == 0)
            def _():
                spread_rest(rs, r_sems)

            @pl.when(core == 1)
            def _():
                for j in range(outs):
                    for c in range(2):
                        left_out(ph, j, c).start()

            lout_ref[ph] = lfull[ph, pl.ds(pl.multiple_of(tenant * rows, rows), rows), :]

            @pl.when(ph == 0)
            def _():
                inverse = split(tab[:, k:])

                def some(i, _):
                    group = range(GROUP)
                    ats = [i * GROUP + j for j in group]
                    lefts = [split(dot3(split(lfull[0, pl.ds(pl.multiple_of(at * rows, rows), rows), :]), inverse, 1, 1))
                             for at in ats]
                    weights = [split(jnp.where(same, dot3(left, left, 1, 1), 0.0)) for left in lefts]
                    for j in group:
                        at = ats[j]
                        cs[1, at // 2, at % 2] = dot3(weights[j], split(rs[at // 2, at % 2]), 1, 0)
                    return 0

                lax.fori_loop(0, nt // GROUP, some, 0)

        return 0

    lax.fori_loop(0, 2, body, 0)

    def keep(ph, at):
        here = pl.ds(pl.multiple_of(at * wq, wq), wq)
        return pltpu.make_async_copy(x.at[ph, here], (fu_hbm, fv_hbm)[ph].at[here], store.at[ph, at])

    def quarter_done(ph, at, inverse):
        here = pl.ds(pl.multiple_of(at * wq, wq), wq)
        x[ph, here, :] = dot3(split(m[ph, at]), inverse, 1, 1)

    near_mine, near_mate = mine, 2 * side + 1 - core

    def fetch_near(ph):
        @pl.when(is_out)
        def _():
            quarter_wait(ph, near_mine)
            quarter_mate(ph, near_mine).start()

    def fetch_far(ph):
        @pl.when(is_out)
        def _():
            at = 2 * (1 - side) + core
            quarter_wait(ph, at)
            quarter_mate(ph, at).start()

    def fetch_rest(ph):
        @pl.when(is_out)
        def _():
            quarter_wait(ph, 2 * (1 - side) + 1 - core)

        @pl.when(is_hub)
        def _():
            quarter_wait(ph, distant[0])

    def fetch_mate(ph):
        @pl.when(jnp.logical_or(core == 1, is_out))
        def _():
            quarter_wait(ph, near_mate)

    def fetch_part(ph):
        @pl.when(is_out)
        def _():
            remote(lout.at[ph], lout.at[ph], lo_send.at[ph, 0, 0], lo_recv.at[ph], mate).wait_recv()
            lout_ref[ph] = lout[ph]

        (fleft_ref, fright_ref)[ph][...] = mm3(lout_ref[ph], linv_ref[ph], 1, 1)

    def give(ph, at):
        quarter_done(ph, at, inverses[ph])
        keep(ph, at).start()

    inverses = [split(linv_ref[ph] * scale) for ph in range(2)]
    for ph in range(2):
        fetch_near(ph)
    fetch_far(0)
    give(0, near_mine)
    give(1, near_mine)
    for ph in range(2):
        fetch_mate(ph)
    fetch_rest(0)
    for at in [near_mate] + distant:
        give(0, at)
    give(1, near_mate)
    fetch_far(1)
    give(1, 2 * (1 - side) + core)
    for ph in range(2):
        fetch_part(ph)
    fetch_rest(1)
    give(1, 2 * (1 - side) + 1 - core)
    ship_end(0)
    ship_end(1)
    spread_end(first, c_sems)
    spread_end(rs, r_sems)

    def drain(ph, _):
        quarter_mate(ph, mine).wait_send()

        @pl.when(is_out)
        def _():
            quarter_mate(ph, 2 * (1 - side) + core).wait_send()

        @pl.when(is_mid)
        def _():
            for j in range(outs):
                quarter_out(ph, j).wait_send()
            left_mate(ph).wait_send()
            left_half(ph).wait_send()
            for d in range(1, n_row):
                left_copy(ph, d).wait_send()
                left_share(ph, d).wait_send()
            left_cross(ph).wait_send()

        @pl.when(is_sub)
        def _():
            gram_mate(ph).wait_send()
            for c in range(2):
                quarter_across(ph, c).wait_send()
                quarter_mate(ph, distant[c]).wait_send()
            for j in range(outs):
                quarter_relay(ph, 0, j).wait_send()

        @pl.when(core == 1)
        def _():
            gram_down(ph).wait_send()

        @pl.when(is_hub)
        def _():
            for j in range(outs):
                gram_out(ph, j).wait_send()
                quarter_relay(ph, 1, j).wait_send()
                for c in range(2):
                    left_out(ph, j, c).wait_send()
            for at in range(nb):
                for part in range(3):
                    gram_copy(ph, at, part).wait_send()

        return 0

    lax.fori_loop(0, 2, drain, 0)
    for ph in range(2):
        for at in range(4):
            keep(ph, at).wait()


def sweep(bits, chain, rank, scale, b, a, u, v):
    rows, width = b.shape
    k = u.shape[1]
    kh, wq = k // 2, width // 4
    nt, n_row = 2 * chain, 1 << bits
    outs, nb = max(chain // 2 - 1, 1), bits + 1
    half = nt * rows // 2
    f32, b16 = jnp.float32, jnp.bfloat16
    dma = pltpu.SemaphoreType.DMA
    big, small = jax.ShapeDtypeStruct((width, k), f32), jax.ShapeDtypeStruct((rows, k), f32)
    return pl.pallas_call(
        functools.partial(sweep_kernel, bits, chain, rank, scale),
        out_shape=(big, big, small, small),
        in_specs=[HBM] * 4,
        out_specs=(ANY, ANY, VMEM, VMEM),
        scratch_shapes=[
            pltpu.VMEM((2, rows, width), f32),
            pltpu.VMEM((2, width, k), f32),
            pltpu.VMEM((bits + 1, 2 * rows, k), f32),
            pltpu.VMEM((bits, 2 * rows, k), f32),
            pltpu.VMEM((2, nt, rows, wq), f32),
            pltpu.VMEM((2, chain, 2, rows, k), f32),
            pltpu.VMEM((chain, 2, rows, k), f32),
            pltpu.VMEM((nt * rows, k), b16),
            pltpu.VMEM((nt * rows, k), b16),
            pltpu.VMEM((wq, k), b16),
            pltpu.VMEM((wq, k), b16),
            pltpu.VMEM((2, 4, wq, k), f32),
            pltpu.VMEM((2, 3, kh, kh), f32),
            pltpu.VMEM((2, 3, kh, kh), f32),
            pltpu.VMEM((2, nb, 3, kh, kh), f32),
            pltpu.VMEM((2, nb, 3, kh, kh), f32),
            pltpu.VMEM((2, 3, kh, kh), f32),
            pltpu.VMEM((2, nt * rows, k), f32),
            pltpu.VMEM((2, half, k), f32),
            pltpu.VMEM((2, n_row, half // n_row, k), f32),
            pltpu.VMEM((2, half // n_row, k), f32),
            pltpu.VMEM((2, nt * rows, k), f32),
            pltpu.VMEM((2, rows, k), f32),
            pltpu.VMEM((k, 2 * k), f32),
            pltpu.VMEM((2, k, k), f32),
            pltpu.VMEM((2, rows, k), f32),
            dma((4,)), dma((2, bits, 2)), dma((2, bits, 2)),
            dma((2, 4)), dma((2, nt)), dma((2,)),
            dma((2,)), dma((chain,)), dma((n_row,)), dma((n_row,)), dma((1,)), dma((1,)),
            dma((2,)), dma((chain,)), dma((n_row,)), dma((n_row,)), dma((1,)), dma((1,)),
            dma((2,)), dma((2,)), dma((2, nb, 3)), dma((2, nb, 3)), dma((2,)), dma((2,)), dma((2, outs)),
            dma((2,)), dma((2,)), dma((2,)), dma((2,)), dma((2, n_row)), dma((2, n_row)), dma((2, n_row)), dma((2, n_row)),
            dma((2,)), dma((2,)), dma((2, outs, 2)), dma((2,)),
            dma((2, outs)), dma((2, 4)), dma((2, 2)), dma((2, 2, outs)), dma((2, 4)), dma((2, 4)),
        ],
        compiler_params=pltpu.CompilerParams(collective_id=0, has_side_effects=True, vmem_limit_bytes=ROOM),
    )(b, a, u, v)


def finish_kernel(u_any, v_any, left_in, right_in, fu_hbm, fv_hbm, left_ref, right_ref, store):
    ins, outs = (u_any, v_any), (fu_hbm, fv_hbm)
    size = u_any.shape[0] // OUT
    spots = [(s, i, pl.ds(i * size, size)) for s in range(2) for i in range(OUT)]
    stores = [pltpu.make_async_copy(ins[s].at[at], outs[s].at[at], store.at[s, i]) for s, i, at in spots]
    for copy in stores:
        copy.start()
    left_ref[...] = left_in[...]
    right_ref[...] = right_in[...]
    for copy in stores:
        copy.wait()


def finish(u, v, left, right):
    big, small = jax.ShapeDtypeStruct(u.shape, u.dtype), jax.ShapeDtypeStruct(left.shape, left.dtype)
    return pl.pallas_call(
        finish_kernel,
        out_shape=(big, big, small, small),
        in_specs=[ANY, ANY, VMEM, VMEM],
        out_specs=(HBM, HBM, VMEM, VMEM),
        scratch_shapes=[pltpu.SemaphoreType.DMA((2, OUT))],
        compiler_params=pltpu.CompilerParams(vmem_limit_bytes=SMALL),
    )(u, v, left, right)


def local(mesh_shape, b_factors, a_factors, u_start, v_start):
    nt, rank, width = b_factors.shape
    rows = nt * rank
    k = u_start.shape[1]
    bits = bits_of(mesh_shape["row"])
    chain = mesh_shape["tenant"] // 2
    scale = math.sqrt(width * mesh_shape["row"])
    arrays = (b_factors.reshape(rows, width), a_factors.reshape(rows, width), u_start, v_start)
    swept = sweep(bits, chain, rank, scale, *(pltpu.with_memory_space_constraint(x, pltpu.HBM) for x in arrays))
    u, v, left, right = finish(*swept)
    return u, v, left.reshape(nt, rank, k), right.reshape(nt, rank, k)


def solution(mesh):
    in_specs = (P("tenant", None, "row"), P("tenant", None, "row"), P("row", None), P("row", None))
    out_specs = (P("row", None), P("row", None), P("tenant", None, None), P("tenant", None, None))
    return jax.shard_map(functools.partial(local, dict(mesh.shape)), mesh=mesh, in_specs=in_specs,
                         out_specs=out_specs, check_vma=False)
```

profile of v0, /device:TPU:0, one launch (start us, length us, event | category | flops | bytes accessed | tf_op | source)
XLA Modules:
  0.0 117.0 jit_solution(16961562333785389453)
XLA Ops:
  0.6 113.6 %shard_map.75 = (f32[2048,256]{1,0:T(8,128)S(1)}, f32[2048,256]{1,0:T(8,128)S(1)}, f32[128,256]{1,0:T(8,128)S(1)}, f32[128,256]{1,0:T(8,128)S(1)}) custom-call(f32[128,2048]{1,0:T(8,128)} %bitcast.4, f32[128,2048]{1,0:T(8,128)} %bitcast.5, f32[2048,256]{1,0:T(8,128)} %u_hbm.1, f32[2048,256]{1,0:T(8,128)} %v_hbm.1), custom_call_target="tpu_custom_call" | custom-call | tf_op jit(solution)/shard_map/pallas_call | solution.py:796
  114.2 2.8 %shard_map.76 = (f32[2048,256]{1,0:T(8,128)}, f32[2048,256]{1,0:T(8,128)}, f32[128,256]{1,0:T(8,128)}, f32[128,256]{1,0:T(8,128)}) custom-call(f32[2048,256]{1,0:T(8,128)S(1)} %get-tuple-element.12.u_any, f32[2048,256]{1,0:T(8,128)S(1)} %get-tuple-element.13.v_any, f32[128,256]{1,0:T(8,128)S(1)} %get-tuple-element.14.left_in, ...), custom_call_target="tpu_custom_call" | custom-call | tf_op jit(solution)/shard_map/pallas_call | solution.py:856
where the time goes:
time: 118 us; the launch traced here: 117 us
  Pallas kernels  116 us (98%)
    pallas_call x1, Pallas kernels, sweep(): pl.pallas_call(functools.partial(sweep_kernel, bits, chain, rank, scale),...  114 us
    pallas_call x1, Pallas kernels, finish(): pl.pallas_call(finish_kernel, out_shape=(big, big, small, small), in_spec...  2.77 us

commit v1 on v0

--- a/solution.py
+++ b/solution.py
@@ -466,10 +466,6 @@
                 spread_meet(first, c_sems)
                 spread_rest(first, c_sems)
 
-            @pl.when(jnp.logical_and(ph == 1, core == 0))
-            def _():
-                relay(0, 0)
-
             own_wait(ph)
             coeffs = cs[ph].reshape(nt * rows, k)
             ctop[...], clow[...] = split(coeffs)
@@ -522,22 +518,41 @@
 
             @pl.when(core == 1)
             def _():
+                @pl.when(ph == 0)
+                def _():
+                    lefts_ready()
+                    for d in order:
+                        left_copy(0, d).start()
+
                 gram_meet(ph, 0)
-                lefts_ready()
+
+                @pl.when(ph == 1)
+                def _():
+                    lefts_ready()
 
                 for at in range(nb):
+                    if at == nb - 1:
+                        @pl.when(ph == 0)
+                        def _():
+                            left_sum(0)
+                            spread_begin(rs, r_sems)
+
                     if at:
                         gram_meet(ph, at)
                     if at == nb - 1:
                         gram_down(ph).start()
                         for j in range(outs):
                             gram_out(ph, j).start()
-                    for d in order[at * share:(at + 1) * share]:
-                        left_copy(ph, d).start()
+
+                    @pl.when(ph == 1)
+                    def _(at=at):
+                        for d in order[at * share:(at + 1) * share]:
+                            left_copy(1, d).start()
 
                 @pl.when(ph == 1)
                 def _():
                     relay_hub(0)
+                    left_sum(1)
 
             @pl.when(core == 0)
             def _():
@@ -546,30 +561,30 @@
                     cross(1)
 
                 lefts_ready()
-
                 for d in order:
                     left_copy(ph, d).start()
 
                 @pl.when(ph == 1)
                 def _():
+                    relay(0, 0)
                     relay(0, 1)
                     relay(1, 0)
 
                 @pl.when(ph == 0)
                 def _():
                     spread_begin(rs, r_sems)
+                    left_sum(0)
                     ship_all(1, far)
 
                 gram_down(ph).wait_recv()
 
+                @pl.when(ph == 1)
+                def _():
+                    left_sum(1)
+
             @pl.when(jnp.logical_and(ph == 0, core == 1))
             def _():
-                spread_begin(rs, r_sems)
-
-            left_sum(ph)
-
-            @pl.when(jnp.logical_and(ph == 0, core == 1))
-            def _():
+                left_join(0)
                 ship_all(1, far)
 
         @pl.when(is_out)
@@ -593,14 +608,14 @@
             if end < k:
                 tab[end:, end:] -= mm(done[:, end - at:k - at], done[:, end - at:], 0, 0)
             if at == BLK:
-                @pl.when(jnp.logical_and(is_mid, ph == 0))
-                def _():
-                    left_join(0)
-
                 @pl.when(jnp.logical_and(is_hub, ph == 1))
                 def _():
                     relay_hub(1)
             if at == 0:
+                @pl.when(jnp.logical_and(is_sub, ph == 0))
+                def _():
+                    left_join(0)
+
                 @pl.when(jnp.logical_and(is_mid, ph == 1))
                 def _():
                     @pl.when(core == 0)
@@ -608,16 +623,13 @@
                         relay(1, 1)
 
                     left_join(1)
+
             if at == 2 * BLK:
                 @pl.when(is_mid)
                 def _():
-                    @pl.when(ph == 0)
+                    @pl.when(jnp.logical_and(ph == 0, core == 0))
                     def _():
-                        spread_meet(rs, r_sems)
-
-                        @pl.when(core == 0)
-                        def _():
-                            cross(0)
+                        cross(0)
         linv_ref[ph] = tab[:, k:]
 
         @pl.when(is_mid)
@@ -626,6 +638,11 @@
                 part = lfull.at[ph, piece_at(neighbour(d))]
                 remote(part, part, ag_send.at[ph, 0], ag_recv.at[ph, neighbour(d)], mate).wait_recv()
             left_half(ph).start()
+
+            @pl.when(ph == 0)
+            def _():
+                spread_meet(rs, r_sems)
+
             left_half(ph).wait_recv()
 
             @pl.when(ph == 0)

time: 118 us -> 116 us (0.983)
  Pallas kernels: 116 us -> 114 us
    pallas_call x1, Pallas kernels: 114 us -> 111 us  [sweep(): pl.pallas_call(functools.partial(sweep_kernel, bits, chain, rank, scale),...]
where the time goes in v1:
time: 116 us; the launch traced here: 115 us
  Pallas kernels  114 us (98%)
    pallas_call x1, Pallas kernels, sweep(): pl.pallas_call(functools.partial(sweep_kernel, bits, chain, rank, scale),...  111 us
    pallas_call x1, Pallas kernels, finish(): pl.pallas_call(finish_kernel, out_shape=(big, big, small, small), in_spec...  2.77 us

profile of v1, /device:TPU:0, one launch (start us, length us, event | category | flops | bytes accessed | tf_op | source)
XLA Modules:
  0.0 114.8 jit_solution(7996388069798027012)
XLA Ops:
  0.6 111.4 %shard_map.75 = (f32[2048,256]{1,0:T(8,128)S(1)}, f32[2048,256]{1,0:T(8,128)S(1)}, f32[128,256]{1,0:T(8,128)S(1)}, f32[128,256]{1,0:T(8,128)S(1)}) custom-call(f32[128,2048]{1,0:T(8,128)} %bitcast.4, f32[128,2048]{1,0:T(8,128)} %bitcast.5, f32[2048,256]{1,0:T(8,128)} %u_hbm.1, f32[2048,256]{1,0:T(8,128)} %v_hbm.1), custom_call_target="tpu_custom_call" | custom-call | tf_op jit(solution)/shard_map/pallas_call | solution.py:813
  112.0 2.8 %shard_map.76 = (f32[2048,256]{1,0:T(8,128)}, f32[2048,256]{1,0:T(8,128)}, f32[128,256]{1,0:T(8,128)}, f32[128,256]{1,0:T(8,128)}) custom-call(f32[2048,256]{1,0:T(8,128)S(1)} %get-tuple-element.12.u_any, f32[2048,256]{1,0:T(8,128)S(1)} %get-tuple-element.13.v_any, f32[128,256]{1,0:T(8,128)S(1)} %get-tuple-element.14.left_in, ...), custom_call_target="tpu_custom_call" | custom-call | tf_op jit(solution)/shard_map/pallas_call | solution.py:873

commit v2 on v1

--- a/solution.py
+++ b/solution.py
@@ -15,10 +15,10 @@
 HBM = pl.BlockSpec(memory_space=pltpu.HBM)
 BLK = 64
 OUT = 4
-WIDE = 128
+WIDE = 256
 ROOM = 44 << 20
 SMALL = 2 << 20
-GROUP = 4
+GROUP = 8
 
 
 def mm(x, y, cx, cy):
@@ -568,6 +568,7 @@
                 def _():
                     relay(0, 0)
                     relay(0, 1)
+                    left_sum(1)
                     relay(1, 0)
 
                 @pl.when(ph == 0)
@@ -577,10 +578,6 @@
                     ship_all(1, far)
 
                 gram_down(ph).wait_recv()
-
-                @pl.when(ph == 1)
-                def _():
-                    left_sum(1)
 
             @pl.when(jnp.logical_and(ph == 0, core == 1))
             def _():
@@ -618,11 +615,11 @@
 
                 @pl.when(jnp.logical_and(is_mid, ph == 1))
                 def _():
+                    left_join(1)
+
                     @pl.when(core == 0)
                     def _():
                         relay(1, 1)
-
-                    left_join(1)
 
             if at == 2 * BLK:
                 @pl.when(is_mid)
@@ -741,10 +738,10 @@
     give(1, near_mate)
     fetch_far(1)
     give(1, 2 * (1 - side) + core)
-    for ph in range(2):
-        fetch_part(ph)
+    fetch_part(0)
     fetch_rest(1)
     give(1, 2 * (1 - side) + 1 - core)
+    fetch_part(1)
     ship_end(0)
     ship_end(1)
     spread_end(first, c_sems)

time: 116 us -> 114 us (0.983)
    pallas_call x1, Pallas kernels: 111 us -> 110 us  [sweep(): pl.pallas_call(functools.partial(sweep_kernel, bits, chain, rank, scale),...]
where the time goes in v2:
time: 114 us; the launch traced here: 113 us
  Pallas kernels  113 us (99%)
    pallas_call x1, Pallas kernels, sweep(): pl.pallas_call(functools.partial(sweep_kernel, bits, chain, rank, scale),...  110 us
    pallas_call x1, Pallas kernels, finish(): pl.pallas_call(finish_kernel, out_shape=(big, big, small, small), in_spec...  2.77 us

profile of v2, /device:TPU:0, one launch (start us, length us, event | category | flops | bytes accessed | tf_op | source)
XLA Modules:
  0.0 113.3 jit_solution(15538861990139682365)
XLA Ops:
  0.6 109.8 %shard_map.75 = (f32[2048,256]{1,0:T(8,128)S(1)}, f32[2048,256]{1,0:T(8,128)S(1)}, f32[128,256]{1,0:T(8,128)S(1)}, f32[128,256]{1,0:T(8,128)S(1)}) custom-call(f32[128,2048]{1,0:T(8,128)} %bitcast.4, f32[128,2048]{1,0:T(8,128)} %bitcast.5, f32[2048,256]{1,0:T(8,128)} %u_hbm.1, f32[2048,256]{1,0:T(8,128)} %v_hbm.1), custom_call_target="tpu_custom_call" | custom-call | tf_op jit(solution)/shard_map/pallas_call | solution.py:810
  110.5 2.8 %shard_map.76 = (f32[2048,256]{1,0:T(8,128)}, f32[2048,256]{1,0:T(8,128)}, f32[128,256]{1,0:T(8,128)}, f32[128,256]{1,0:T(8,128)}) custom-call(f32[2048,256]{1,0:T(8,128)S(1)} %get-tuple-element.12.u_any, f32[2048,256]{1,0:T(8,128)S(1)} %get-tuple-element.13.v_any, f32[128,256]{1,0:T(8,128)S(1)} %get-tuple-element.14.left_in, ...), custom_call_target="tpu_custom_call" | custom-call | tf_op jit(solution)/shard_map/pallas_call | solution.py:870

commit v3 on v2

--- a/solution.py
+++ b/solution.py
@@ -15,7 +15,7 @@
 HBM = pl.BlockSpec(memory_space=pltpu.HBM)
 BLK = 64
 OUT = 4
-WIDE = 256
+WIDE = 512
 ROOM = 44 << 20
 SMALL = 2 << 20
 GROUP = 8
@@ -155,6 +155,7 @@
     half = nt * rows // 2
     piece = half // n_row
     mine = 2 * side + core
+    wide = min(WIDE, wq)
 
     def outer(j):
         return (1 - side) * (low - 1 - j) + side * (low + 2 + j)
@@ -471,15 +472,15 @@
             ctop[...], clow[...] = split(coeffs)
 
             def columns(j, _):
-                cols = pl.ds(pl.multiple_of(j * WIDE, WIDE), WIDE)
-                here = pl.ds(pl.multiple_of(j * WIDE, WIDE), WIDE)
-                block = own[ph, :, :, cols].reshape(nt * rows, WIDE)
+                cols = pl.ds(pl.multiple_of(j * wide, wide), wide)
+                here = pl.ds(pl.multiple_of(j * wide, wide), wide)
+                block = own[ph, :, :, cols].reshape(nt * rows, wide)
                 total = dot3(split(block), (ctop[...], clow[...]), 0, 0)
                 m[ph, mine, here, :] = total
                 mtop[here, :], mlow[here, :] = split(total)
                 return 0
 
-            lax.fori_loop(0, wq // WIDE, columns, 0)
+            lax.fori_loop(0, wq // wide, columns, 0)
             for j in range(outs):
                 quarter_out(ph, j).start()
             quarter_mate(ph, mine).start()

time: 114 us -> 114 us (level)
  no operation moved by 1% of the time
where the time goes in v3:
time: 114 us
  Pallas kernels  113 us (99%)
    pallas_call x1, Pallas kernels, sweep(): pl.pallas_call(functools.partial(sweep_kernel, bits, chain, rank, scale),...  110 us
    pallas_call x1, Pallas kernels, finish(): pl.pallas_call(finish_kernel, out_shape=(big, big, small, small), in_spec...  2.77 us

profile of v3, /device:TPU:0, one launch (start us, length us, event | category | flops | bytes accessed | tf_op | source)
XLA Modules:
  0.0 113.6 jit_solution(2316187348161015201)
XLA Ops:
  0.6 110.0 %shard_map.75 = (f32[2048,256]{1,0:T(8,128)S(1)}, f32[2048,256]{1,0:T(8,128)S(1)}, f32[128,256]{1,0:T(8,128)S(1)}, f32[128,256]{1,0:T(8,128)S(1)}) custom-call(f32[128,2048]{1,0:T(8,128)} %bitcast.4, f32[128,2048]{1,0:T(8,128)} %bitcast.5, f32[2048,256]{1,0:T(8,128)} %u_hbm.1, f32[2048,256]{1,0:T(8,128)} %v_hbm.1), custom_call_target="tpu_custom_call" | custom-call | tf_op jit(solution)/shard_map/pallas_call | solution.py:811
  110.6 2.8 %shard_map.76 = (f32[2048,256]{1,0:T(8,128)}, f32[2048,256]{1,0:T(8,128)}, f32[128,256]{1,0:T(8,128)}, f32[128,256]{1,0:T(8,128)}) custom-call(f32[2048,256]{1,0:T(8,128)S(1)} %get-tuple-element.12.u_any, f32[2048,256]{1,0:T(8,128)S(1)} %get-tuple-element.13.v_any, f32[128,256]{1,0:T(8,128)S(1)} %get-tuple-element.14.left_in, ...), custom_call_target="tpu_custom_call" | custom-call | tf_op jit(solution)/shard_map/pallas_call | solution.py:871
